TPU v7x, 512 devices: a whole 4x8x8 slice. The times are simulated.
512 devices in a mesh: col: 128 (over y, z, core), lev: 4 (over x).
Axes of the slice: x: 4, y: 8, z: 8, core: 2. Of those that a mesh axis runs over, the one named last changes fastest.
Arguments:
- fields: bfloat16 [2, 32, 131072], P(None, 'lev', 'col'), may hold values from 0.5 to 3
- bracket: int32 [8, 131072], P(None, 'col'), may hold values from 0 to 30
- fraction: float32 [8, 131072], P(None, 'col'), may hold values from 0 to 1
- remap_weights: bfloat16 [2048, 128, 128], P('col'), may hold values from 0 to 0.015625
- intersections: int32 [3, 4096], P(None, 'col'), may hold values from 0 to 1023, as said below
- tile_owner: int32 [1024], replicated, may hold values from 0 to 1023, as said below
Outputs:
- normalized: float32 [2, 8, 1024, 128], P(None, 'lev', 'col')
Inputs may be any that keep to these rules, and one draw needn't show every extreme that they name: `intersections`: row 0 names a source block of the entry's own col index; row 1 a target tile whose owner, tile_owner[tile] // 8, lies within 2 indices of the entry's col index or exactly 64 indices away, cyclically; row 2 a weight block of the entry's own col index. `tile_owner`: A permutation of the tiles.
All inputs are finite; a program needn't handle non-finite values.
Results may differ from a plain program's by a relative error of at most 0.00031.
Values may be sent and summed in bfloat16 or wider, within the bound.
No kernel may reach another device: no remote copies, remote signals or barrier semaphores. Data moves between devices by JAX's collectives and lax.ppermute only.
A program may use at most 64 MiB of HBM per device.

v0:
```python
import jax
import jax.numpy as jnp
from jax import lax
from jax.sharding import PartitionSpec as P

F = 2
PLEV = 8
epsilon = 1e-06


def mix_levels(level_block, lower_level, weight_up):
    level_ids = jnp.arange(level_block.shape[1], dtype=jnp.int32)
    is_below = level_ids[None, :, None] == lower_level[:, None, :]
    is_above = level_ids[None, :, None] == lower_level[:, None, :] + 1
    level_coef = jnp.where(
        is_below, 1.0 - weight_up[:, None, :], jnp.where(is_above, weight_up[:, None, :], 0.0)
    )
    return jnp.sum(level_coef[None] * level_block.astype(jnp.float32)[:, None], axis=2)


def gather_rows(selector, partial_tiles):
    return lax.dot_general(
        selector,
        partial_tiles,
        (((0,), (0,)), ((), ())),
        precision=lax.Precision.HIGHEST,
        preferred_element_type=jnp.float32,
    )


def per_device(fields, bracket, fraction, remap_weights, intersections, tile_owner):
    lev_index = lax.axis_index("lev")
    plev_dev = PLEV // lax.axis_size("lev")
    column_levels = lax.all_gather(fields, "lev", axis=1, tiled=True)
    lower_level = lax.dynamic_slice_in_dim(bracket, lev_index * plev_dev, plev_dev, 0)
    weight_up = lax.dynamic_slice_in_dim(fraction, lev_index * plev_dev, plev_dev, 0)
    interp = mix_levels(column_levels, lower_level, weight_up).astype(jnp.bfloat16)
    block_cols = remap_weights.shape[1]
    tile_cells = remap_weights.shape[2]
    blocks = interp.reshape(F, plev_dev, -1, block_cols)
    chosen = jnp.take(blocks, intersections[0], axis=2)
    picked = jnp.take(remap_weights, intersections[2], axis=0)
    partial_tiles = jnp.einsum("fpeb,ebt->efpt", chosen, picked, preferred_element_type=jnp.float32)
    entries = partial_tiles.shape[0]
    partial_tiles = partial_tiles.reshape(entries, -1)
    tile_total = tile_owner.shape[0]
    col_count = lax.axis_size("col")
    tile_dev = tile_total // col_count
    matches = intersections[1][:, None] == jnp.arange(tile_total, dtype=jnp.int32)[None, :]
    slot_index = jnp.sum(jnp.where(matches, tile_owner[None, :], 0), axis=1)
    selector = (
        slot_index[:, None] == jnp.arange(tile_dev * lax.axis_size("col"), dtype=jnp.int32)[None, :]
    ).astype(jnp.float32)
    remapped = lax.psum_scatter(
        gather_rows(selector, partial_tiles), "col", scatter_dimension=0, tiled=True
    )
    remapped = remapped.reshape(tile_dev, F, plev_dev, tile_cells).transpose(1, 2, 0, 3)
    shifted_left = jnp.concatenate([remapped[..., :1], remapped[..., :-1]], axis=-1)
    shifted_right = jnp.concatenate([remapped[..., 1:], remapped[..., -1:]], axis=-1)
    filtered = 0.25 * shifted_left + 0.5 * remapped + 0.25 * shifted_right
    cells = float(tile_dev * tile_cells * col_count)
    local_sums = jnp.sum(filtered, axis=(2, 3))
    field_mean = lax.psum(local_sums, "col") / cells
    centered = filtered - field_mean[:, :, None, None]
    field_var = lax.psum(jnp.sum(centered * centered, axis=(2, 3)), "col") / cells
    return centered * lax.rsqrt(field_var + epsilon)[:, :, None, None]


def solution(mesh):
    in_specs = (
        P(None, "lev", "col"),
        P(None, "col"),
        P(None, "col"),
        P("col", None, None),
        P(None, "col"),
        P(),
    )
    out_specs = P(None, "lev", "col", None)
    return jax.shard_map(
        per_device, mesh=mesh, in_specs=in_specs, out_specs=out_specs, check_vma=False
    )
```

profile of v0, /device:TPU:1, one launch (start us, length us, event | category | flops | bytes accessed | tf_op | source)
XLA Modules:
  0.0 736.7 jit_solution(11726878282647201093)
XLA Ops:
  6.5 0.0 copy-start
  6.5 0.0 reduce-scatter.2.cloned.1.call-start
  6.5 0.7 slice_bitcast_fusion
  7.3 0.8 fusion.11
  8.0 0.8 compare_and_fusion.1
  8.8 0.8 broadcast_add_fusion
  9.6 0.8 broadcast_subtract_fusion
  10.3 10.5 %all_gather.3 = bf16[2,32,1024]{2,1,0:T(8,128)(2,1)S(1)} all-gather(bf16[2,8,1024]{2,1,0:T(8,128)(2,1)} %param.6), channel_id=1, replica_groups=mesh['col'=128,'lev'=4] {'lev'}, dimensions={1}, use_global_device_ids=true | all-gather | bytes 163840 | tf_op jit(solution)/shard_map/all_gather | solution.py:34
  20.9 0.1 multiply_reduce_fusion
  21.0 0.0 copy-start.1
  21.0 0.6 gather_fusion
  21.6 0.0 copy-done
  21.6 0.7 gather_fusion.1
  22.4 0.5 fusion
  22.9 0.1 reshape.97
  22.9 0.0 copy-done.1
  22.9 0.2 select_reduce_fusion
  23.1 2.5 fusion.5
  25.6 0.0 reduce-scatter.2.cloned.1.call-update
  25.6 202.3 %reduce-scatter.2.cloned.1.call-done = f32[8,512]{1,0:T(8,128)} async-done(((f32[1024,512]{1,0:T(8,128)}), f32[8,512]{1,0:T(8,128)}) %reduce-scatter.2.cloned.1.call-update) | async-done | bytes 16400 | tf_op jit(solution)/shard_map/reduce_scatter | solution.py:54
  227.9 0.9 fusion.17
  228.8 0.9 fusion.16
  229.6 0.9 fusion.14
  230.5 251.6 %psum.14 = f32[2,2]{1,0:T(2,128)S(1)} all-reduce(f32[2,2]{1,0:T(2,128)S(1)} %get-tuple-element.5), channel_id=1, replica_groups=mesh['col'=128,'lev'=4] {'col'}, use_global_device_ids=true, to_apply=%region_4.5 | all-reduce | flops 4 | bytes 32 | tf_op jit(solution)/shard_map/psum | solution.py:63
  482.2 0.2 multiply_reduce_fusion.1
  482.3 246.8 %psum.15 = f32[2,2]{1,0:T(2,128)S(1)} all-reduce(f32[2,2]{1,0:T(2,128)S(1)} %multiply_reduce_fusion.1), channel_id=1, replica_groups=mesh['col'=128,'lev'=4] {'col'}, use_global_device_ids=true, to_apply=%region_6.7 | all-reduce | flops 4 | bytes 32 | tf_op jit(solution)/shard_map/psum | solution.py:65
  729.1 0.7 subtract_multiply_fusion
  (5 shorter events, 0.1 us)
Async XLA Ops:
  6.5 15.1 %copy-start = (bf16[16,128,128]{2,1,0:T(8,128)(2,1)S(1)}, bf16[16,128,128]{2,1,0:T(8,128)(2,1)}, u32[]{:S(2)}) copy-start(bf16[16,128,128]{2,1,0:T(8,128)(2,1)} %param.9) | copy-start | bytes 1572868
  6.5 221.4 %reduce-scatter.2.cloned.1.call-start = ((), (), s32[]{:S(2)}) async-start(), calls=%async_computation.1 | async-start | bytes 2113536 | tf_op jit(solution)/shard_map/reduce_scatter | solution.py:54
  21.0 1.9 copy-start.1
Sparse Core Ops, SparseCore 0:
  25.7 202.1 reduce-scatter.1
where the time goes:
time: 737 us
  blocking collectives  509 us (69%)
  waiting for transfers between devices  202 us (27%)
  between operations  13.5 us (2%)
    psum x1, blocking collectives, per_device(): field_mean = lax.psum(local_sums, 'col') / cells  252 us
    psum x1, blocking collectives, per_device(): lax.psum(jnp.sum(centered * centered, axis=(2, 3)), 'col') / cells  247 us
    reduce_scatter x1, waiting for transfers between devices, per_device(): lax.psum_scatter(gather_rows(selector, partial_tiles), 'col', scatter_dim...  202 us
  transfers between devices with their start and end apart: 1, of which 1 were waited for; matrix products, arithmetic and copies ran while one was open for 0% of the time, Pallas kernels for 0%

commit v1 on v0

--- a/solution.py
+++ b/solution.py
@@ -6,6 +6,10 @@
 F = 2
 PLEV = 8
 epsilon = 1e-06
+
+
+def finish_groups(arr):
+    return lax.all_gather(arr, "col").sum(axis=0)
 
 
 def mix_levels(level_block, lower_level, weight_up):
@@ -60,7 +64,7 @@
     filtered = 0.25 * shifted_left + 0.5 * remapped + 0.25 * shifted_right
     cells = float(tile_dev * tile_cells * col_count)
     local_sums = jnp.sum(filtered, axis=(2, 3))
-    field_mean = lax.psum(local_sums, "col") / cells
+    field_mean = finish_groups(local_sums) / cells
     centered = filtered - field_mean[:, :, None, None]
     field_var = lax.psum(jnp.sum(centered * centered, axis=(2, 3)), "col") / cells
     return centered * lax.rsqrt(field_var + epsilon)[:, :, None, None]

time: 737 us -> 541 us (0.73)
  blocking collectives: 509 us -> 311 us
    psum x1 -> x0, blocking collectives: 252 us -> none  [per_device(): field_mean = lax.psum(local_sums, 'col') / cells]
    all_gather x0 -> x1, blocking collectives: none -> 53.9 us  [finish_groups(): return lax.all_gather(arr, 'col').sum(axis=0)]
where the time goes in v1:
time: 541 us; the launch traced here: 539 us
  blocking collectives  311 us (57%)
  waiting for transfers between devices  202 us (37%)
  between operations  13.5 us (2%)
    psum x1, blocking collectives, per_device(): lax.psum(jnp.sum(centered * centered, axis=(2, 3)), 'col') / cells  246 us
    reduce_scatter x1, waiting for transfers between devices, per_device(): lax.psum_scatter(gather_rows(selector, partial_tiles), 'col', scatter_dim...  202 us
    all_gather x1, blocking collectives, finish_groups(): return lax.all_gather(arr, 'col').sum(axis=0)  53.9 us
  transfers between devices with their start and end apart: 1, of which 1 were waited for; matrix products, arithmetic and copies ran while one was open for 0% of the time, Pallas kernels for 0%

profile of v1, /device:TPU:1, one launch (start us, length us, event | category | flops | bytes accessed | tf_op | source)
XLA Modules:
  0.0 538.6 jit_solution(3085503436206874832)
XLA Ops:
  6.5 0.0 copy-start
  6.5 0.0 reduce-scatter.2.cloned.1.call-start
  6.5 0.7 slice_bitcast_fusion
  7.3 0.8 fusion.11
  8.0 0.8 compare_and_fusion.1
  8.8 0.8 broadcast_add_fusion
  9.6 0.8 broadcast_subtract_fusion
  10.3 10.5 %all_gather.9 = bf16[2,32,1024]{2,1,0:T(8,128)(2,1)S(1)} all-gather(bf16[2,8,1024]{2,1,0:T(8,128)(2,1)} %param.6), channel_id=1, replica_groups=mesh['col'=128,'lev'=4] {'lev'}, dimensions={1}, use_global_device_ids=true | all-gather | bytes 163840 | tf_op jit(solution)/shard_map/all_gather | solution.py:38
  20.9 0.1 multiply_reduce_fusion
  21.0 0.0 copy-start.1
  21.0 0.6 gather_fusion
  21.6 0.0 copy-done
  21.6 0.7 gather_fusion.1
  22.4 0.5 fusion
  22.9 0.1 reshape.99
  22.9 0.0 copy-done.1
  22.9 0.2 select_reduce_fusion
  23.1 2.5 fusion.5
  25.6 0.0 reduce-scatter.2.cloned.1.call-update
  25.6 202.3 %reduce-scatter.2.cloned.1.call-done = f32[8,512]{1,0:T(8,128)} async-done(((f32[1024,512]{1,0:T(8,128)}), f32[8,512]{1,0:T(8,128)}) %reduce-scatter.2.cloned.1.call-update) | async-done | bytes 16400 | tf_op jit(solution)/shard_map/reduce_scatter | solution.py:58
  227.9 0.9 fusion.17
  228.8 0.9 fusion.16
  229.6 0.9 fusion.14
  230.5 53.9 %all-gather.1 = f32[128,2,2]{2,1,0:T(2,128)S(1)} all-gather(f32[1,2,2]{2,1,0:T(2,128)S(1)} %bitcast.34), channel_id=2, replica_groups=mesh['col'=128,'lev'=4] {'col'}, dimensions={0}, use_global_device_ids=true | all-gather | bytes 2064 | tf_op jit(solution)/shard_map/all_gather | solution.py:12
  284.4 0.1 reduce_sum.48
  284.6 0.2 multiply_reduce_fusion.1
  284.7 246.3 %psum.7 = f32[2,2]{1,0:T(2,128)S(1)} all-reduce(f32[2,2]{1,0:T(2,128)S(1)} %multiply_reduce_fusion.1), channel_id=1, replica_groups=mesh['col'=128,'lev'=4] {'col'}, use_global_device_ids=true, to_apply=%region_6.7 | all-reduce | flops 4 | bytes 32 | tf_op jit(solution)/shard_map/psum | solution.py:69
  531.1 0.7 subtract_multiply_fusion
  (5 shorter events, 0.1 us)
Async XLA Ops:
  6.5 15.1 %copy-start = (bf16[16,128,128]{2,1,0:T(8,128)(2,1)S(1)}, bf16[16,128,128]{2,1,0:T(8,128)(2,1)}, u32[]{:S(2)}) copy-start(bf16[16,128,128]{2,1,0:T(8,128)(2,1)} %param.9) | copy-start | bytes 1572868
  6.5 221.4 %reduce-scatter.2.cloned.1.call-start = ((), (), s32[]{:S(2)}) async-start(), calls=%async_computation.1 | async-start | bytes 2113536 | tf_op jit(solution)/shard_map/reduce_scatter | solution.py:58
  21.0 1.9 copy-start.1
Sparse Core Ops, SparseCore 0:
  25.7 202.1 reduce-scatter.1
